TPU v7x, 256 devices: a whole 4x4x8 slice. The times are simulated.
256 devices in a mesh: term: 8 (over z), sec: 32 (over y, x, core).
Axes of the slice: x: 4, y: 4, z: 8, core: 2. Of those that a mesh axis runs over, the one named last changes fastest.
Arguments:
- start_vectors: bfloat16 [2, 64, 256, 256], P(None, 'sec'), may hold values from -6 to 6
- left_env: bfloat16 [32, 64, 256, 256], P('term', 'sec'), may hold values from -0.375 to 0.375
- right_env: bfloat16 [32, 64, 256, 256], P('term', 'sec'), may hold values from -0.375 to 0.375
- term_shift: int32 [32], P('term'), may hold values from -1 to 1
- precond: float32 [64, 256, 256], P('sec'), may hold values from 0.25 to 4
- block_dims: int32 [64], P('sec'), may hold values from 1 to 256, 8192 in all
Outputs:
- vector: float32 [2, 64, 256, 256], P(None, 'sec', 'term')
- energy: float32 [2], replicated
Inputs may be any that keep to these rules, and one draw needn't show every extreme that they name: `block_dims`: one block has exactly 256 live states.
All inputs are finite; a program needn't handle non-finite values.
Results may differ from a plain program's by a relative error of at most 0.0036.
Values may be sent and summed in bfloat16 or wider, within the bound.
No kernel may reach another device: no remote copies, remote signals or barrier semaphores. Data moves between devices by JAX's collectives and lax.ppermute only.
A program may use at most 64 MiB of HBM per device.

v0:
```python
import jax
import jax.numpy as jnp
from jax import lax
from jax.sharding import PartitionSpec as P

ITERS = 2


def padded(x, sides, width):
    for axis, dim in sides:
        count, length = (lax.axis_size(axis), x.shape[dim])
        up = [(i, (i + 1) % count) for i in range(count - 1)]
        down = [(j, i) for i, j in up]
        last = lax.slice_in_dim(x, length - width, length, axis=dim)
        initial = lax.slice_in_dim(x, 0, width, axis=dim)
        before = lax.ppermute(last, axis, up)
        after = lax.ppermute(initial, axis, down)
        x = jnp.concatenate([before, x, after], axis=dim)
    return x


def shards(start_vectors, left_env, right_env, term_shift, precond, block_dims):
    vec_count, blocks, states, _ = start_vectors.shape
    groups = lax.axis_size("term")
    share = states // groups
    offset_row = lax.axis_index("term") * share
    factor = 1.0 / (blocks * lax.axis_size("sec") * states * states)
    position = jnp.arange(states, dtype=jnp.int32)
    live_rows = position[None, :, None] < block_dims[:, None, None]
    live_cols = position[None, None, :] < block_dims[:, None, None]
    mask = (live_rows & live_cols).astype(jnp.float32)
    shift_sel = term_shift[:, None, None, None, None]

    def apply_op(vector_bf):
        local = jnp.einsum(
            "ujab,kjcb->kujac", vector_bf, right_env, preferred_element_type=jnp.float32
        ).astype(jnp.bfloat16)
        wide = padded(local, (("sec", 2),), 1)
        chosen = jnp.where(
            shift_sel < 0,
            wide[:, :, 0:blocks],
            jnp.where(shift_sel == 0, wide[:, :, 1 : blocks + 1], wide[:, :, 2 : blocks + 2]),
        )
        partial_sum = (
            jnp.einsum("kbac,kubcd->ubad", left_env, chosen, preferred_element_type=jnp.float32)
            * mask
        )
        result = lax.psum(partial_sum, "term")
        return result

    def totals(values):
        result = lax.psum(values, "sec")
        return result

    def inner(left, right):
        return jnp.sum(left * right, axis=(1, 2, 3)) * factor

    def expand(value):
        return value[:, None, None, None]

    start = start_vectors * mask.astype(jnp.bfloat16)
    h_vec = apply_op(start)
    vector = start.astype(jnp.float32)
    pre_view = precond[None]
    length = jnp.sqrt(totals(inner(vector, vector)[None])[0] + 1e-06)
    vector = vector / expand(length)
    h_vec = h_vec / expand(length)
    energy = jnp.zeros((vec_count,), jnp.float32)
    for iteration in range(ITERS):
        rayleigh = totals(inner(vector, h_vec)[None])[0]
        resid = h_vec - expand(rayleigh) * vector
        precon_res = pre_view * resid
        correlation = totals(inner(vector, precon_res)[None])[0]
        direction = precon_res - expand(correlation) * vector
        pair = totals(jnp.stack([inner(direction, direction), inner(direction, h_vec)]))
        square, raw_coupling = (pair[0], pair[1])
        dir_norm = jnp.sqrt(square + 1e-06)
        coupling = raw_coupling / dir_norm
        direction = direction / expand(dir_norm)
        widen_result = direction.astype(jnp.bfloat16)
        h_dir = apply_op(widen_result)
        curvature = totals(inner(direction, h_dir)[None])[0]
        energy = 0.5 * (rayleigh + curvature) - jnp.sqrt(
            (0.5 * (rayleigh - curvature)) ** 2 + coupling**2
        )
        weight = energy - rayleigh
        new_size = jnp.sqrt(coupling**2 + weight**2)
        vector = (expand(coupling) * vector + expand(weight) * direction) / expand(new_size)
        h_vec = (expand(coupling) * h_vec + expand(weight) * h_dir) / expand(new_size)
    final = lax.dynamic_slice_in_dim(vector, offset_row, share, 2)
    return (final, energy)


def solution(mesh):
    return jax.shard_map(
        shards,
        mesh=mesh,
        in_specs=(
            P(None, "sec", None, None),
            P("term", "sec", None, None),
            P("term", "sec", None, None),
            P("term"),
            P("sec", None, None),
            P("sec"),
        ),
        out_specs=(P(None, "sec", "term", None), P()),
        check_vma=False,
    )
```

profile of v0, /device:TPU:1, one launch (start us, length us, event | category | flops | bytes accessed | tf_op | source)
XLA Modules:
  0.0 827.7 jit_solution(5210906045877564215)
XLA Ops:
  10.7 4.6 collective-permute-start
  17.3 9.7 %collective-permute-done = bf16[4,2,1,256,256]{4,3,0,1,2:T(8,128)(2,1)S(1)} collective-permute-done((bf16[4,2,1,256,256]{4,3,0,1,2:T(8,128)(2,1)S(1)}, bf16[4,2,1,256,256]{4,3,0,1,2:T(8,128)(2,1)S(1)}, u32[]{:S(2)}, u32[]{:S(2)}) %collective-permute-start) | collective-permute-done | bytes 1048608 | tf_op jit(solution)/shard_map/ppermute | solution.py:16
  27.1 4.4 collective-permute-done.1
  31.5 2.4 fusion.27
  34.3 61.0 %psum.85 = f32[1,2]{1,0:T(1,128)S(1)} all-reduce(f32[1,2]{1,0:T(1,128)S(1)} %multiply_bitcast_fusion.6), channel_id=1, replica_groups=mesh['term'=8,'sec'=32] {'sec'}, use_global_device_ids=true, to_apply=%region_2.3 | all-reduce | flops 2 | bytes 16 | tf_op jit(solution)/shard_map/psum | solution.py:52
  95.3 14.4 %all-reduce.4.cloned.1.call-done = f32[2,2,256,256]{2,3,0,1:T(8,128)} async-done(((f32[2,2,256,256]{2,3,0,1:T(8,128)}), f32[2,2,256,256]{2,3,0,1:T(8,128)}) %all-reduce.4.cloned.1.call-update) | async-done | bytes 1048592 | tf_op jit(solution)/shard_map/psum | solution.py:48
  112.6 67.1 %psum.86 = f32[2]{0:T(128)S(1)} all-reduce(f32[2]{0:T(128)S(1)} %broadcast_multiply_fusion.5), channel_id=1, replica_groups=mesh['term'=8,'sec'=32] {'sec'}, use_global_device_ids=true, to_apply=%region_4.5 | all-reduce | flops 2 | bytes 16 | tf_op jit(solution)/shard_map/psum | solution.py:52
  180.2 62.7 %psum.87 = f32[2]{0:T(128)S(1)} all-reduce(f32[2]{0:T(128)S(1)} %broadcast_multiply_fusion.4), channel_id=1, replica_groups=mesh['term'=8,'sec'=32] {'sec'}, use_global_device_ids=true, to_apply=%region_6.7 | all-reduce | flops 2 | bytes 16 | tf_op jit(solution)/shard_map/psum | solution.py:52
  244.5 62.7 %psum.88 = f32[2,2]{1,0:T(2,128)S(1)} all-reduce(f32[2,2]{1,0:T(2,128)S(1)} %pad_maximum_fusion.9), channel_id=1, replica_groups=mesh['term'=8,'sec'=32] {'sec'}, use_global_device_ids=true, to_apply=%region_9.10 | all-reduce | flops 4 | bytes 32 | tf_op jit(solution)/shard_map/psum | solution.py:52
  311.6 2.5 collective-permute-start.3
  314.0 9.2 %collective-permute-done.2 = bf16[4,2,1,256,256]{4,3,0,1,2:T(8,128)(2,1)S(1)} collective-permute-done((bf16[4,2,1,256,256]{4,3,0,1,2:T(8,128)(2,1)S(1)}, bf16[4,2,1,256,256]{4,3,0,1,2:T(8,128)(2,1)S(1)}, u32[]{:S(2)}, u32[]{:S(2)}) %collective-permute-start.2) | collective-permute-done | bytes 1048608 | tf_op jit(solution)/shard_map/ppermute | solution.py:16
  323.3 4.4 collective-permute-done.3
  330.1 65.6 %all-reduce.6.cloned.1.call-done = f32[2,2,256,256]{2,3,0,1:T(8,128)} async-done(((f32[2,2,256,256]{2,3,0,1:T(8,128)}), f32[2,2,256,256]{2,3,0,1:T(8,128)}) %all-reduce.6.cloned.1.call-update) | async-done | bytes 1048592 | tf_op jit(solution)/shard_map/psum | solution.py:48
  397.7 67.1 %psum.90 = f32[2]{0:T(128)S(1)} all-reduce(f32[2]{0:T(128)S(1)} %broadcast_multiply_fusion.3), channel_id=1, replica_groups=mesh['term'=8,'sec'=32] {'sec'}, use_global_device_ids=true, to_apply=%region_12.13 | all-reduce | flops 2 | bytes 16 | tf_op jit(solution)/shard_map/psum | solution.py:52
  464.8 3.5 multiply_reduce_fusion.4
  468.3 62.8 %psum.91 = f32[2]{0:T(128)S(1)} all-reduce(f32[2]{0:T(128)S(1)} %broadcast_multiply_fusion.2), channel_id=1, replica_groups=mesh['term'=8,'sec'=32] {'sec'}, use_global_device_ids=true, to_apply=%region_14.15 | all-reduce | flops 2 | bytes 16 | tf_op jit(solution)/shard_map/psum | solution.py:52
  533.0 62.7 %psum.92 = f32[2]{0:T(128)S(1)} all-reduce(f32[2]{0:T(128)S(1)} %broadcast_multiply_fusion.1), channel_id=1, replica_groups=mesh['term'=8,'sec'=32] {'sec'}, use_global_device_ids=true, to_apply=%region_16.17 | all-reduce | flops 2 | bytes 16 | tf_op jit(solution)/shard_map/psum | solution.py:52
  595.6 2.6 multiply_reduce_fusion.2
  598.2 62.7 %psum.93 = f32[2,2]{1,0:T(2,128)S(1)} all-reduce(f32[2,2]{1,0:T(2,128)S(1)} %pad_maximum_fusion.10), channel_id=1, replica_groups=mesh['term'=8,'sec'=32] {'sec'}, use_global_device_ids=true, to_apply=%region_19.20 | all-reduce | flops 4 | bytes 32 | tf_op jit(solution)/shard_map/psum | solution.py:52
  665.6 2.5 collective-permute-start.5
  668.1 9.2 %collective-permute-done.4 = bf16[4,2,1,256,256]{4,3,0,1,2:T(8,128)(2,1)S(1)} collective-permute-done((bf16[4,2,1,256,256]{4,3,0,1,2:T(8,128)(2,1)S(1)}, bf16[4,2,1,256,256]{4,3,0,1,2:T(8,128)(2,1)S(1)}, u32[]{:S(2)}, u32[]{:S(2)}) %collective-permute-start.4) | collective-permute-done | bytes 1048608 | tf_op jit(solution)/shard_map/ppermute | solution.py:16
  677.3 4.4 collective-permute-done.5
  684.1 65.3 %all-reduce.8.cloned.1.call-done = f32[2,2,256,256]{2,3,0,1:T(8,128)} async-done(((f32[2,2,256,256]{2,3,0,1:T(8,128)}), f32[2,2,256,256]{2,3,0,1:T(8,128)}) %all-reduce.8.cloned.1.call-update) | async-done | bytes 1048592 | tf_op jit(solution)/shard_map/psum | solution.py:48
  751.3 67.1 %psum.95 = f32[2]{0:T(128)S(1)} all-reduce(f32[2]{0:T(128)S(1)} %broadcast_multiply_fusion), channel_id=1, replica_groups=mesh['term'=8,'sec'=32] {'sec'}, use_global_device_ids=true, to_apply=%region_22.23 | all-reduce | flops 2 | bytes 16 | tf_op jit(solution)/shard_map/psum | solution.py:52
  (71 shorter events, 33.1 us)
Async XLA Ops:
  7.2 2.5 copy-start
  7.2 102.5 %all-reduce.4.cloned.1.call-start = ((), (), s32[]{:S(2)}) async-start(), calls=%async_computation | async-start | bytes 2097152 | tf_op jit(solution)/shard_map/psum | solution.py:48
  8.2 23.3 %copy-start.4 = (f32[2,256,256]{1,2,0:T(8,128)}, f32[2,256,256]{1,2,0:T(8,128)S(1)}, u32[]{:S(2)}) copy-start(f32[2,256,256]{1,2,0:T(8,128)S(1)} %get-tuple-element.26) | copy-start | bytes 1572868
  10.5 6.8 copy-start.10
  10.5 21.0 %copy-start.7 = (bf16[4,2,256,256]{3,2,1,0:T(8,128)(2,1)S(1)}, bf16[4,2,256,256]{3,2,1,0:T(8,128)(2,1)}, u32[]{:S(2)}) copy-start(bf16[4,2,256,256]{3,2,1,0:T(8,128)(2,1)} %param.7) | copy-start | bytes 3145732
  10.7 16.4 %collective-permute-start = (bf16[4,2,1,256,256]{4,3,0,1,2:T(8,128)(2,1)S(1)}, bf16[4,2,1,256,256]{4,3,0,1,2:T(8,128)(2,1)S(1)}, u32[]{:S(2)}, u32[]{:S(2)}) collective-permute-start(bf16[4,2,1,256,256]{4,3,0,1,2:T(8,128)(2,1)S(1)} %get-tuple-element.24), channel_id=1, source_target_pairs={{0,1},{1,2},{2,3},{3,4},{4,5},{5,6},{6,7},{7,8},{8,9},{9,10},{10,1... | collective-permute-start | bytes 3145736 | tf_op jit(solution)/shard_map/ppermute | solution.py:16
  15.3 16.1 %collective-permute-start.1 = (bf16[4,2,1,256,256]{4,3,0,1,2:T(8,128)(2,1)S(1)}, bf16[4,2,1,256,256]{4,3,0,1,2:T(8,128)(2,1)S(1)}, u32[]{:S(2)}, u32[]{:S(2)}) collective-permute-start(bf16[4,2,1,256,256]{4,3,0,1,2:T(8,128)(2,1)S(1)} %get-tuple-element.25), channel_id=1, source_target_pairs={{1,0},{2,1},{3,2},{4,3},{5,4},{6,5},{7,6},{8,7},{9,8},{10,9},{11,1... | collective-permute-start | bytes 3145736 | tf_op jit(solution)/shard_map/ppermute | solution.py:17
  33.9 361.9 %all-reduce.6.cloned.1.call-start = ((), (), s32[]{:S(2)}) async-start(), calls=%async_computation.1 | async-start | bytes 2097152 | tf_op jit(solution)/shard_map/psum | solution.py:48
  109.7 70.1 %copy-start.1 = (f32[2,2,256,256]{2,3,0,1:T(8,128)S(1)}, f32[2,2,256,256]{2,3,0,1:T(8,128)}, u32[]{:S(2)}) copy-start(f32[2,2,256,256]{2,3,0,1:T(8,128)} %all-reduce.4.cloned.1.call-done) | copy-start | bytes 3145732
  309.3 18.4 %copy-start.5 = (f32[2,256,256]{1,2,0:T(8,128)S(1)}, f32[2,256,256]{1,2,0:T(8,128)}, u32[]{:S(2)}) copy-start(f32[2,256,256]{1,2,0:T(8,128)} %copy-done.4) | copy-start | bytes 1572868
  309.3 18.4 %copy-start.8 = (bf16[4,2,256,256]{3,2,1,0:T(8,128)(2,1)S(1)}, bf16[4,2,256,256]{3,2,1,0:T(8,128)(2,1)}, u32[]{:S(2)}) copy-start(bf16[4,2,256,256]{3,2,1,0:T(8,128)(2,1)} %param.7) | copy-start | bytes 3145732
  309.5 13.8 %collective-permute-start.2 = (bf16[4,2,1,256,256]{4,3,0,1,2:T(8,128)(2,1)S(1)}, bf16[4,2,1,256,256]{4,3,0,1,2:T(8,128)(2,1)S(1)}, u32[]{:S(2)}, u32[]{:S(2)}) collective-permute-start(bf16[4,2,1,256,256]{4,3,0,1,2:T(8,128)(2,1)S(1)} %get-tuple-element.22), channel_id=1, source_target_pairs={{0,1},{1,2},{2,3},{3,4},{4,5},{5,6},{6,7},{7,8},{8,9},{9,10},{10,1... | collective-permute-start | bytes 3145736 | tf_op jit(solution)/shard_map/ppermute | solution.py:16
  311.6 16.1 %collective-permute-start.3 = (bf16[4,2,1,256,256]{4,3,0,1,2:T(8,128)(2,1)S(1)}, bf16[4,2,1,256,256]{4,3,0,1,2:T(8,128)(2,1)S(1)}, u32[]{:S(2)}, u32[]{:S(2)}) collective-permute-start(bf16[4,2,1,256,256]{4,3,0,1,2:T(8,128)(2,1)S(1)} %get-tuple-element.23), channel_id=1, source_target_pairs={{1,0},{2,1},{3,2},{4,3},{5,4},{6,5},{7,6},{8,7},{9,8},{10,9},{11,1... | collective-permute-start | bytes 3145736 | tf_op jit(solution)/shard_map/ppermute | solution.py:17
  330.1 419.3 %all-reduce.8.cloned.1.call-start = ((), (), s32[]{:S(2)}) async-start(), calls=%async_computation.2 | async-start | bytes 2097152 | tf_op jit(solution)/shard_map/psum | solution.py:48
  468.3 127.4 %copy-start.2 = (f32[2,2,256,256]{2,3,0,1:T(8,128)S(1)}, f32[2,2,256,256]{2,3,0,1:T(8,128)}, u32[]{:S(2)}) copy-start(f32[2,2,256,256]{2,3,0,1:T(8,128)} %get-tuple-element.15) | copy-start | bytes 3145732
  662.3 1.0 copy-start.3
  663.4 18.4 %copy-start.6 = (f32[2,256,256]{1,2,0:T(8,128)S(1)}, f32[2,256,256]{1,2,0:T(8,128)}, u32[]{:S(2)}) copy-start(f32[2,256,256]{1,2,0:T(8,128)} %copy-done.4) | copy-start | bytes 1572868
  663.4 18.4 %copy-start.9 = (bf16[4,2,256,256]{3,2,1,0:T(8,128)(2,1)S(1)}, bf16[4,2,256,256]{3,2,1,0:T(8,128)(2,1)}, u32[]{:S(2)}) copy-start(bf16[4,2,256,256]{3,2,1,0:T(8,128)(2,1)} %param.7) | copy-start | bytes 3145732
  663.5 13.8 %collective-permute-start.4 = (bf16[4,2,1,256,256]{4,3,0,1,2:T(8,128)(2,1)S(1)}, bf16[4,2,1,256,256]{4,3,0,1,2:T(8,128)(2,1)S(1)}, u32[]{:S(2)}, u32[]{:S(2)}) collective-permute-start(bf16[4,2,1,256,256]{4,3,0,1,2:T(8,128)(2,1)S(1)} %get-tuple-element.20), channel_id=1, source_target_pairs={{0,1},{1,2},{2,3},{3,4},{4,5},{5,6},{6,7},{7,8},{8,9},{9,10},{10,1... | collective-permute-start | bytes 3145736 | tf_op jit(solution)/shard_map/ppermute | solution.py:16
  665.6 16.1 %collective-permute-start.5 = (bf16[4,2,1,256,256]{4,3,0,1,2:T(8,128)(2,1)S(1)}, bf16[4,2,1,256,256]{4,3,0,1,2:T(8,128)(2,1)S(1)}, u32[]{:S(2)}, u32[]{:S(2)}) collective-permute-start(bf16[4,2,1,256,256]{4,3,0,1,2:T(8,128)(2,1)S(1)} %get-tuple-element.21), channel_id=1, source_target_pairs={{1,0},{2,1},{3,2},{4,3},{5,4},{6,5},{7,6},{8,7},{9,8},{10,9},{11,1... | collective-permute-start | bytes 3145736 | tf_op jit(solution)/shard_map/ppermute | solution.py:17
Sparse Core Ops, SparseCore 0:
  34.0 75.5 all-reduce.3
  330.2 65.5 all-reduce.5
  684.2 65.1 all-reduce.7
where the time goes:
time: 829 us; the launch traced here: 828 us
  blocking collectives  576 us (69%)
  waiting for transfers between devices  187 us (23%)
  other arithmetic  20.1 us (2%)
  starting transfers between devices  15.8 us (2%)
  between operations  14 us (2%)
  matrix products  11 us (1%)
    psum x9, blocking collectives, totals(): result = lax.psum(values, 'sec')  576 us
    psum x3, waiting for transfers between devices, apply_op(): result = lax.psum(partial_sum, 'term')  145 us
    ppermute x3, waiting for transfers between devices, padded(): before = lax.ppermute(last, axis, up)  28.2 us
  transfers between devices with their start and end apart: 9, of which 9 were waited for; matrix products, arithmetic and copies ran while one was open for 0% of the time, Pallas kernels for 0%

commit v1 on v0

--- a/solution.py
+++ b/solution.py
@@ -4,6 +4,14 @@
 from jax.sharding import PartitionSpec as P
 
 ITERS = 2
+
+
+def added_up(array, mesh_axis):
+    count, total = (lax.axis_size(mesh_axis), array)
+    for stride in [1 << k for k in range(count.bit_length() - 1)]:
+        pairs = [(i, i ^ stride) for i in range(count)]
+        total = total + lax.ppermute(total, mesh_axis, pairs)
+    return total
 
 
 def padded(x, sides, width):
@@ -49,7 +57,7 @@
         return result
 
     def totals(values):
-        result = lax.psum(values, "sec")
+        result = added_up(values, "sec")
         return result
 
     def inner(left, right):

time: 829 us -> 487 us (0.59)
  the two profiles are of different devices: /device:TPU:1 before, /device:TPU:2 now
where the time goes in v1:
time: 487 us; the launch traced here: 478 us
  waiting for transfers between devices  352 us (72%)
  starting transfers between devices  86.8 us (18%)
  between operations  14.5 us (3%)
  other arithmetic  11.4 us (2%)
  matrix products  9.71 us (2%)
    psum x3, waiting for transfers between devices, apply_op(): result = lax.psum(partial_sum, 'term')  216 us
    ppermute x45, waiting for transfers between devices, added_up(): total = total + lax.ppermute(total, mesh_axis, pairs)  99.4 us
    ppermute x45, starting transfers between devices, added_up(): total = total + lax.ppermute(total, mesh_axis, pairs)  69.5 us
    ppermute x3, waiting for transfers between devices, padded(): before = lax.ppermute(last, axis, up)  31.6 us
    ppermute x3, starting transfers between devices, padded(): after = lax.ppermute(initial, axis, down)  10.9 us
  transfers between devices with their start and end apart: 54, of which 54 were waited for; matrix products, arithmetic and copies ran while one was open for 0% of the time, Pallas kernels for 0%

profile of v1, /device:TPU:2, one launch (start us, length us, event | category | flops | bytes accessed | tf_op | source)
XLA Modules:
  0.0 478.0 jit_solution(5922897029188140077)
XLA Ops:
  12.8 3.6 collective-permute-start.1
  16.4 10.5 %collective-permute-done = bf16[4,2,1,256,256]{4,3,0,1,2:T(8,128)(2,1)S(1)} collective-permute-done((bf16[4,2,1,256,256]{4,3,0,1,2:T(8,128)(2,1)S(1)}, bf16[4,2,1,256,256]{4,3,0,1,2:T(8,128)(2,1)S(1)}, u32[]{:S(2)}, u32[]{:S(2)}) %collective-permute-start) | collective-permute-done | bytes 1048608 | tf_op jit(solution)/shard_map/ppermute | solution.py:24
  34.6 3.0 collective-permute-done.3
  37.7 4.2 collective-permute-start.4
  52.1 61.1 %all-reduce.4.cloned.1.call-done = f32[2,2,256,256]{2,3,0,1:T(8,128)} async-done(((f32[2,2,256,256]{2,3,0,1:T(8,128)}), f32[2,2,256,256]{2,3,0,1:T(8,128)}) %all-reduce.4.cloned.1.call-update) | async-done | bytes 1048592 | tf_op jit(solution)/shard_map/psum | solution.py:56
  121.7 3.0 collective-permute-done.9
  128.3 3.0 collective-permute-start.11
  140.7 3.0 collective-permute-done.14
  147.4 3.0 collective-permute-start.16
  160.4 3.0 collective-permute-done.19
  167.0 3.0 collective-permute-start.21
  175.3 3.6 collective-permute-start.23
  178.9 10.5 %collective-permute-done.22 = bf16[4,2,1,256,256]{4,3,0,1,2:T(8,128)(2,1)S(1)} collective-permute-done((bf16[4,2,1,256,256]{4,3,0,1,2:T(8,128)(2,1)S(1)}, bf16[4,2,1,256,256]{4,3,0,1,2:T(8,128)(2,1)S(1)}, u32[]{:S(2)}, u32[]{:S(2)}) %collective-permute-start.22) | collective-permute-done | bytes 1048608 | tf_op jit(solution)/shard_map/ppermute | solution.py:24
  193.7 77.5 %all-reduce.6.cloned.1.call-done = f32[2,2,256,256]{2,3,0,1:T(8,128)} async-done(((f32[2,2,256,256]{2,3,0,1:T(8,128)}), f32[2,2,256,256]{2,3,0,1:T(8,128)}) %all-reduce.6.cloned.1.call-update) | async-done | bytes 1048592 | tf_op jit(solution)/shard_map/psum | solution.py:56
  280.1 3.0 collective-permute-done.26
  286.7 3.0 collective-permute-start.28
  306.3 3.0 collective-permute-start.33
  325.3 3.0 collective-permute-start.38
  338.2 3.0 collective-permute-done.41
  344.8 3.0 collective-permute-start.43
  353.3 3.6 collective-permute-start.45
  357.0 10.5 %collective-permute-done.44 = bf16[4,2,1,256,256]{4,3,0,1,2:T(8,128)(2,1)S(1)} collective-permute-done((bf16[4,2,1,256,256]{4,3,0,1,2:T(8,128)(2,1)S(1)}, bf16[4,2,1,256,256]{4,3,0,1,2:T(8,128)(2,1)S(1)}, u32[]{:S(2)}, u32[]{:S(2)}) %collective-permute-start.44) | collective-permute-done | bytes 1048608 | tf_op jit(solution)/shard_map/ppermute | solution.py:24
  371.7 77.5 %all-reduce.8.cloned.1.call-done = f32[2,2,256,256]{2,3,0,1:T(8,128)} async-done(((f32[2,2,256,256]{2,3,0,1:T(8,128)}), f32[2,2,256,256]{2,3,0,1:T(8,128)}) %all-reduce.8.cloned.1.call-update) | async-done | bytes 1048592 | tf_op jit(solution)/shard_map/psum | solution.py:56
  464.3 3.0 collective-permute-start.50
  (206 shorter events, 158.5 us)
Async XLA Ops:
  7.2 106.0 %all-reduce.4.cloned.1.call-start = ((), (), s32[]{:S(2)}) async-start(), calls=%async_computation | async-start | bytes 2097152 | tf_op jit(solution)/shard_map/psum | solution.py:56
  10.7 16.2 %collective-permute-start = (bf16[4,2,1,256,256]{4,3,0,1,2:T(8,128)(2,1)S(1)}, bf16[4,2,1,256,256]{4,3,0,1,2:T(8,128)(2,1)S(1)}, u32[]{:S(2)}, u32[]{:S(2)}) collective-permute-start(bf16[4,2,1,256,256]{4,3,0,1,2:T(8,128)(2,1)S(1)} %get-tuple-element.24), channel_id=1, source_target_pairs={{0,1},{1,2},{2,3},{3,4},{4,5},{5,6},{6,7},{7,8},{8,9},{9,10},{10,1... | collective-permute-start | bytes 3145736 | tf_op jit(solution)/shard_map/ppermute | solution.py:24
  12.8 15.9 %collective-permute-start.1 = (bf16[4,2,1,256,256]{4,3,0,1,2:T(8,128)(2,1)S(1)}, bf16[4,2,1,256,256]{4,3,0,1,2:T(8,128)(2,1)S(1)}, u32[]{:S(2)}, u32[]{:S(2)}) collective-permute-start(bf16[4,2,1,256,256]{4,3,0,1,2:T(8,128)(2,1)S(1)} %get-tuple-element.25), channel_id=1, source_target_pairs={{1,0},{2,1},{3,2},{4,3},{5,4},{6,5},{7,6},{8,7},{9,8},{10,9},{11,1... | collective-permute-start | bytes 3145736 | tf_op jit(solution)/shard_map/ppermute | solution.py:25
  31.1 240.1 %all-reduce.6.cloned.1.call-start = ((), (), s32[]{:S(2)}) async-start(), calls=%async_computation.1 | async-start | bytes 2097152 | tf_op jit(solution)/shard_map/psum | solution.py:56
  37.7 5.8 %collective-permute-start.4 = (f32[1,2]{1,0:T(1,128)S(1)}, f32[1,2]{1,0:T(1,128)S(1)}, u32[]{:S(2)}, u32[]{:S(2)}) collective-permute-start(f32[1,2]{1,0:T(1,128)S(1)} %add.250), channel_id=1, source_target_pairs={{0,4},{1,5},{2,6},{3,7},{4,0},{5,1},{6,2},{7,3},{8,12},{9,13},{10,... | collective-permute-start | bytes 32 | tf_op jit(solution)/shard_map/ppermute | solution.py:13
  47.0 5.1 %collective-permute-start.6 = (f32[1,2]{1,0:T(1,128)S(1)}, f32[1,2]{1,0:T(1,128)S(1)}, u32[]{:S(2)}, u32[]{:S(2)}) collective-permute-start(f32[1,2]{1,0:T(1,128)S(1)} %add.252), channel_id=1, source_target_pairs={{0,16},{1,17},{2,18},{3,19},{4,20},{5,21},{6,22},{7,23},{8,24},{9,... | collective-permute-start | bytes 32 | tf_op jit(solution)/shard_map/ppermute | solution.py:13
  119.6 5.1 %collective-permute-start.9 = (f32[1,2]{1,0:T(1,128)S(1)}, f32[1,2]{1,0:T(1,128)S(1)}, u32[]{:S(2)}, u32[]{:S(2)}) collective-permute-start(f32[1,2]{1,0:T(1,128)S(1)} %add.256), channel_id=1, source_target_pairs={{0,4},{1,5},{2,6},{3,7},{4,0},{5,1},{6,2},{7,3},{8,12},{9,13},{10,... | collective-permute-start | bytes 32 | tf_op jit(solution)/shard_map/ppermute | solution.py:13
  128.3 5.1 %collective-permute-start.11 = (f32[1,2]{1,0:T(1,128)S(1)}, f32[1,2]{1,0:T(1,128)S(1)}, u32[]{:S(2)}, u32[]{:S(2)}) collective-permute-start(f32[1,2]{1,0:T(1,128)S(1)} %add.258), channel_id=1, source_target_pairs={{0,16},{1,17},{2,18},{3,19},{4,20},{5,21},{6,22},{7,23},{8,24},{9,... | collective-permute-start | bytes 32 | tf_op jit(solution)/shard_map/ppermute | solution.py:13
  138.6 5.1 %collective-permute-start.14 = (f32[1,2]{1,0:T(1,128)S(1)}, f32[1,2]{1,0:T(1,128)S(1)}, u32[]{:S(2)}, u32[]{:S(2)}) collective-permute-start(f32[1,2]{1,0:T(1,128)S(1)} %add.261), channel_id=1, source_target_pairs={{0,4},{1,5},{2,6},{3,7},{4,0},{5,1},{6,2},{7,3},{8,12},{9,13},{10,... | collective-permute-start | bytes 32 | tf_op jit(solution)/shard_map/ppermute | solution.py:13
  147.4 5.1 %collective-permute-start.16 = (f32[1,2]{1,0:T(1,128)S(1)}, f32[1,2]{1,0:T(1,128)S(1)}, u32[]{:S(2)}, u32[]{:S(2)}) collective-permute-start(f32[1,2]{1,0:T(1,128)S(1)} %add.263), channel_id=1, source_target_pairs={{0,16},{1,17},{2,18},{3,19},{4,20},{5,21},{6,22},{7,23},{8,24},{9,... | collective-permute-start | bytes 32 | tf_op jit(solution)/shard_map/ppermute | solution.py:13
  158.3 5.2 %collective-permute-start.19 = (f32[2,2]{1,0:T(2,128)S(1)}, f32[2,2]{1,0:T(2,128)S(1)}, u32[]{:S(2)}, u32[]{:S(2)}) collective-permute-start(f32[2,2]{1,0:T(2,128)S(1)} %fusion.88), channel_id=1, source_target_pairs={{0,4},{1,5},{2,6},{3,7},{4,0},{5,1},{6,2},{7,3},{8,12},{9,13},{10,... | collective-permute-start | bytes 56 | tf_op jit(solution)/shard_map/ppermute | solution.py:13
  167.0 5.1 %collective-permute-start.21 = (f32[2,2]{1,0:T(2,128)S(1)}, f32[2,2]{1,0:T(2,128)S(1)}, u32[]{:S(2)}, u32[]{:S(2)}) collective-permute-start(f32[2,2]{1,0:T(2,128)S(1)} %add.268), channel_id=1, source_target_pairs={{0,16},{1,17},{2,18},{3,19},{4,20},{5,21},{6,22},{7,23},{8,24},{9,... | collective-permute-start | bytes 56 | tf_op jit(solution)/shard_map/ppermute | solution.py:13
  173.2 16.2 %collective-permute-start.22 = (bf16[4,2,1,256,256]{4,3,0,1,2:T(8,128)(2,1)S(1)}, bf16[4,2,1,256,256]{4,3,0,1,2:T(8,128)(2,1)S(1)}, u32[]{:S(2)}, u32[]{:S(2)}) collective-permute-start(bf16[4,2,1,256,256]{4,3,0,1,2:T(8,128)(2,1)S(1)} %get-tuple-element.22), channel_id=1, source_target_pairs={{0,1},{1,2},{2,3},{3,4},{4,5},{5,6},{6,7},{7,8},{8,9},{9,10},{10,1... | collective-permute-start | bytes 3145736 | tf_op jit(solution)/shard_map/ppermute | solution.py:24
  175.3 15.9 %collective-permute-start.23 = (bf16[4,2,1,256,256]{4,3,0,1,2:T(8,128)(2,1)S(1)}, bf16[4,2,1,256,256]{4,3,0,1,2:T(8,128)(2,1)S(1)}, u32[]{:S(2)}, u32[]{:S(2)}) collective-permute-start(bf16[4,2,1,256,256]{4,3,0,1,2:T(8,128)(2,1)S(1)} %get-tuple-element.23), channel_id=1, source_target_pairs={{1,0},{2,1},{3,2},{4,3},{5,4},{6,5},{7,6},{8,7},{9,8},{10,9},{11,1... | collective-permute-start | bytes 3145736 | tf_op jit(solution)/shard_map/ppermute | solution.py:25
  193.6 255.6 %all-reduce.8.cloned.1.call-start = ((), (), s32[]{:S(2)}) async-start(), calls=%async_computation.2 | async-start | bytes 2097152 | tf_op jit(solution)/shard_map/psum | solution.py:56
  278.0 5.1 %collective-permute-start.26 = (f32[1,2]{1,0:T(1,128)S(1)}, f32[1,2]{1,0:T(1,128)S(1)}, u32[]{:S(2)}, u32[]{:S(2)}) collective-permute-start(f32[1,2]{1,0:T(1,128)S(1)} %add.272), channel_id=1, source_target_pairs={{0,4},{1,5},{2,6},{3,7},{4,0},{5,1},{6,2},{7,3},{8,12},{9,13},{10,... | collective-permute-start | bytes 32 | tf_op jit(solution)/shard_map/ppermute | solution.py:13
  286.7 5.1 %collective-permute-start.28 = (f32[1,2]{1,0:T(1,128)S(1)}, f32[1,2]{1,0:T(1,128)S(1)}, u32[]{:S(2)}, u32[]{:S(2)}) collective-permute-start(f32[1,2]{1,0:T(1,128)S(1)} %add.274), channel_id=1, source_target_pairs={{0,16},{1,17},{2,18},{3,19},{4,20},{5,21},{6,22},{7,23},{8,24},{9,... | collective-permute-start | bytes 32 | tf_op jit(solution)/shard_map/ppermute | solution.py:13
  297.5 5.3 %collective-permute-start.31 = (f32[1,2]{1,0:T(1,128)S(1)}, f32[1,2]{1,0:T(1,128)S(1)}, u32[]{:S(2)}, u32[]{:S(2)}) collective-permute-start(f32[1,2]{1,0:T(1,128)S(1)} %add.282), channel_id=1, source_target_pairs={{0,4},{1,5},{2,6},{3,7},{4,0},{5,1},{6,2},{7,3},{8,12},{9,13},{10,... | collective-permute-start | bytes 32 | tf_op jit(solution)/shard_map/ppermute | solution.py:13
  306.3 5.1 %collective-permute-start.33 = (f32[1,2]{1,0:T(1,128)S(1)}, f32[1,2]{1,0:T(1,128)S(1)}, u32[]{:S(2)}, u32[]{:S(2)}) collective-permute-start(f32[1,2]{1,0:T(1,128)S(1)} %add.284), channel_id=1, source_target_pairs={{0,16},{1,17},{2,18},{3,19},{4,20},{5,21},{6,22},{7,23},{8,24},{9,... | collective-permute-start | bytes 32 | tf_op jit(solution)/shard_map/ppermute | solution.py:13
  316.6 5.1 %collective-permute-start.36 = (f32[1,2]{1,0:T(1,128)S(1)}, f32[1,2]{1,0:T(1,128)S(1)}, u32[]{:S(2)}, u32[]{:S(2)}) collective-permute-start(f32[1,2]{1,0:T(1,128)S(1)} %add.287), channel_id=1, source_target_pairs={{0,4},{1,5},{2,6},{3,7},{4,0},{5,1},{6,2},{7,3},{8,12},{9,13},{10,... | collective-permute-start | bytes 32 | tf_op jit(solution)/shard_map/ppermute | solution.py:13
  336.0 5.2 %collective-permute-start.41 = (f32[2,2]{1,0:T(2,128)S(1)}, f32[2,2]{1,0:T(2,128)S(1)}, u32[]{:S(2)}, u32[]{:S(2)}) collective-permute-start(f32[2,2]{1,0:T(2,128)S(1)} %fusion.87), channel_id=1, source_target_pairs={{0,4},{1,5},{2,6},{3,7},{4,0},{5,1},{6,2},{7,3},{8,12},{9,13},{10,... | collective-permute-start | bytes 56 | tf_op jit(solution)/shard_map/ppermute | solution.py:13
  344.8 5.1 %collective-permute-start.43 = (f32[2,2]{1,0:T(2,128)S(1)}, f32[2,2]{1,0:T(2,128)S(1)}, u32[]{:S(2)}, u32[]{:S(2)}) collective-permute-start(f32[2,2]{1,0:T(2,128)S(1)} %add.294), channel_id=1, source_target_pairs={{0,16},{1,17},{2,18},{3,19},{4,20},{5,21},{6,22},{7,23},{8,24},{9,... | collective-permute-start | bytes 56 | tf_op jit(solution)/shard_map/ppermute | solution.py:13
  351.3 16.2 %collective-permute-start.44 = (bf16[4,2,1,256,256]{4,3,0,1,2:T(8,128)(2,1)S(1)}, bf16[4,2,1,256,256]{4,3,0,1,2:T(8,128)(2,1)S(1)}, u32[]{:S(2)}, u32[]{:S(2)}) collective-permute-start(bf16[4,2,1,256,256]{4,3,0,1,2:T(8,128)(2,1)S(1)} %get-tuple-element.20), channel_id=1, source_target_pairs={{0,1},{1,2},{2,3},{3,4},{4,5},{5,6},{6,7},{7,8},{8,9},{9,10},{10,1... | collective-permute-start | bytes 3145736 | tf_op jit(solution)/shard_map/ppermute | solution.py:24
  353.3 15.9 %collective-permute-start.45 = (bf16[4,2,1,256,256]{4,3,0,1,2:T(8,128)(2,1)S(1)}, bf16[4,2,1,256,256]{4,3,0,1,2:T(8,128)(2,1)S(1)}, u32[]{:S(2)}, u32[]{:S(2)}) collective-permute-start(bf16[4,2,1,256,256]{4,3,0,1,2:T(8,128)(2,1)S(1)} %get-tuple-element.21), channel_id=1, source_target_pairs={{1,0},{2,1},{3,2},{4,3},{5,4},{6,5},{7,6},{8,7},{9,8},{10,9},{11,1... | collective-permute-start | bytes 3145736 | tf_op jit(solution)/shard_map/ppermute | solution.py:25
  (47 other events, 453.6 us)
Sparse Core Ops, SparseCore 0:
  31.2 81.8 all-reduce.3
  193.8 77.4 all-reduce.5
  371.8 77.3 all-reduce.7
